TPU v7x, 512 devices: a whole 4x4x16 slice. The times are simulated.
512 devices in a mesh: dp: 32 (over y, x, core), table: 16 (over z).
Axes of the slice: x: 4, y: 4, z: 16, core: 2. Of those that a mesh axis runs over, the one named last changes fastest.
Arguments:
- hidden_in: bfloat16 [4096, 4096], P('dp', 'table'), may hold values from -6 to 6
- gate_weight: bfloat16 [4096, 4096], P('dp', 'table'), may hold values from -0.09375 to 0.09375
- values: bfloat16 [2048, 4096], P('table'), may hold values from -6 to 6
- pick_rows: int32 [4096, 32], P('dp'), may hold values from 0 to 2047, all different within a row
- pick_scores: float32 [4096, 32], P('dp'), may hold values from -300 to 300
- grad_out: bfloat16 [4096, 4096], P('dp', 'table'), may hold values from -6 to 6
Outputs:
- branch_out: bfloat16 [4096, 4096], P('dp', 'table')
- grad_hidden: bfloat16 [4096, 4096], P('dp', 'table')
- grad_gate: float32 [4096, 4096], P('dp', 'table')
- grad_values: float32 [2048, 4096], P('table')
- grad_scores: float32 [4096, 32], P('dp')
Inputs may be any that keep to these rules, and one draw needn't show every extreme that they name: `pick_rows`: the 32 rows of a token are distinct.
All inputs are finite; a program needn't handle non-finite values.
Results may differ from a plain program's by a relative error of at most 0.025.
Values may be sent and summed in bfloat16 or wider, within the bound.
A program may use at most 64 MiB of HBM per device.

v0:
```python
import jax
import jax.numpy as jnp
from jax import lax
from jax.sharding import PartitionSpec as P


def pick_weights(pick_scores):
    row_max = jnp.max(pick_scores, axis=1, keepdims=True)
    exponent = jnp.exp(pick_scores - row_max)
    return exponent / jnp.sum(exponent, axis=1, keepdims=True)


def spread_weights(row_ids, weights_bf, row_total):
    token_ids = lax.broadcasted_iota(jnp.int32, row_ids.shape, 0)
    empty = jnp.zeros((row_ids.shape[0], row_total), jnp.bfloat16)
    return empty.at[token_ids, row_ids].set(weights_bf, mode="drop")


def local(hidden_in, gate_weight, values, pick_rows, pick_scores, grad_out):
    weights = pick_weights(pick_scores)
    weights_bf = weights.astype(jnp.bfloat16)
    token_count = hidden_in.shape[0]
    col_count = hidden_in.shape[1]
    rows_here = values.shape[0]
    whole_in = lax.all_gather(hidden_in, "table", axis=1, tiled=True)
    weight_full = lax.all_gather(gate_weight, "dp", axis=0, tiled=True)
    local_rows = pick_rows - lax.axis_index("table") * rows_here
    owned = (local_rows >= 0) & (local_rows < rows_here)
    parked = jnp.where(owned, local_rows, rows_here)
    spread = spread_weights(parked, weights_bf, rows_here)
    partial_mem = jnp.dot(spread, values, preferred_element_type=jnp.float32)
    arrived = lax.all_to_all(
        partial_mem.astype(jnp.bfloat16), "table", split_axis=1, concat_axis=0, tiled=True
    ).astype(partial_mem.dtype)
    memory_read = jnp.sum(arrived.reshape(-1, token_count, col_count), axis=0)
    gate_input = jnp.dot(whole_in, weight_full, preferred_element_type=jnp.float32)
    sigmoid_v = jax.nn.sigmoid(gate_input)
    gate_value = gate_input * sigmoid_v
    gate_slope = sigmoid_v * (1.0 + gate_input * (1.0 - sigmoid_v))
    branch_out = (memory_read * gate_value).astype(jnp.bfloat16)
    upstream = grad_out.astype(jnp.float32)
    mem_grad = (upstream * gate_value).astype(jnp.bfloat16)
    gate_grad_in = (upstream * memory_read * gate_slope).astype(jnp.bfloat16)
    grad_full = lax.all_gather(mem_grad, "table", axis=1, tiled=True)
    value_term = lax.dot_general(
        spread, grad_full, (((0,), (0,)), ((), ())), preferred_element_type=jnp.float32
    )
    affinity_all = lax.dot_general(
        grad_full, values, (((1,), (1,)), ((), ())), preferred_element_type=jnp.float32
    )
    picked = jnp.take_along_axis(affinity_all, jnp.where(owned, local_rows, 0), axis=1)
    affinity_part = jnp.where(owned, picked, 0.0)
    affinity = lax.psum(affinity_part, "table")
    grad_scores = weights * (affinity - jnp.sum(weights * affinity, axis=1, keepdims=True))
    grad_values = lax.psum(value_term.astype(jnp.bfloat16), "dp").astype(jnp.float32)
    grad_gate = lax.psum_scatter(
        lax.dot_general(
            whole_in, gate_grad_in, (((0,), (0,)), ((), ())), preferred_element_type=jnp.float32
        ).astype(jnp.bfloat16),
        "dp",
        scatter_dimension=0,
        tiled=True,
    ).astype(jnp.float32)
    input_term = lax.dot_general(
        gate_grad_in, weight_full, (((1,), (1,)), ((), ())), preferred_element_type=jnp.float32
    )
    grad_hidden = lax.psum_scatter(
        input_term.astype(jnp.bfloat16), "table", scatter_dimension=1, tiled=True
    )
    return (branch_out, grad_hidden, grad_gate, grad_values, grad_scores)


def solution(mesh):
    placed = (
        P("dp", "table"),
        P("dp", "table"),
        P("table", None),
        P("dp", None),
        P("dp", None),
        P("dp", "table"),
    )
    return jax.shard_map(
        local,
        mesh=mesh,
        in_specs=placed,
        out_specs=(
            P("dp", "table"),
            P("dp", "table"),
            P("dp", "table"),
            P("table", None),
            P("dp", None),
        ),
        check_vma=False,
    )
```

profile of v0, /device:TPU:6, one launch (start us, length us, event | category | flops | bytes accessed | tf_op | source)
XLA Modules:
  0.0 570.6 jit_solution(2590282525393934483)
XLA Ops:
  7.2 0.7 all-gather.4.cloned.1.call-update
  7.9 0.8 copy.22
  8.9 0.7 multiply_reduce_fusion.1
  9.8 0.8 copy.25
  10.6 0.7 reduce_max.9
  11.3 0.2 fusion.7
  11.7 28.6 %scatter_custom_fusion = bf16[16384]{0:T(1024)(128)(2,1)S(1)} fusion(s32[4096]{0:T(1024)S(1)} %reshape.49, bf16[4096]{0:T(1024)(128)(2,1)S(1)} %reshape.51, bf16[]{:T(256)} %constant.9.clone.1), kind=kCustom, calls=%fused_computation.33 | custom fusion | bytes 32770
  40.4 0.4 convolution_convert_fusion.3
  40.8 1.1 copy.33
  41.9 15.3 %all-to-all-start = ((bf16[128,16,256]{2,0,1:T(8,128)(2,1)}), bf16[128,16,256]{2,0,1:T(8,128)(2,1)S(1)}, u32[]{:S(2)}, u32[]{:S(2)}) async-start(bf16[128,16,256]{2,0,1:T(8,128)(2,1)} %bitcast.27), calls=%async_computation | async-start | bytes 2097152 | tf_op jit(solution)/shard_map/all_to_all | solution.py:32
  57.3 0.7 all-gather.6.cloned.1.call-update
  58.0 54.4 %all-to-all-done = bf16[128,16,256]{2,0,1:T(8,128)(2,1)S(1)} async-done(((bf16[128,16,256]{2,0,1:T(8,128)(2,1)}), bf16[128,16,256]{2,0,1:T(8,128)(2,1)S(1)}, u32[]{:S(2)}, u32[]{:S(2)}) %all-to-all-start) | async-done | bytes 1048608 | tf_op jit(solution)/shard_map/all_to_all | solution.py:32
  112.4 0.1 convert_reduce_fusion
  112.5 1.2 all-gather.4.cloned.1.call-done
  113.8 59.5 %all-gather.6.cloned.1.call-done = bf16[4096,256]{1,0:T(8,128)(2,1)} async-done(((bf16[128,256]{1,0:T(8,128)(2,1)}), bf16[4096,256]{1,0:T(8,128)(2,1)}) %all-gather.6.cloned.1.call-update) | async-done | bytes 2097168 | tf_op jit(solution)/shard_map/all_gather | solution.py:26
  173.3 3.1 fusion.2
  176.4 72.2 %all-gather.8.cloned.1.call-done = bf16[128,4096]{1,0:T(8,128)(2,1)} async-done(((bf16[128,256]{1,0:T(8,128)(2,1)}), bf16[128,4096]{1,0:T(8,128)(2,1)}) %all-gather.8.cloned.1.call-update) | async-done | bytes 1048592 | tf_op jit(solution)/shard_map/all_gather | solution.py:44
  248.6 2.7 convolution_convert_fusion.1
  251.3 1.9 fusion
  253.3 2.5 copy.29
  255.8 3.5 convolution_convert_fusion.2
  259.5 0.4 fusion.13
  259.9 25.6 %gather_fusion = f32[4096]{0:T(1024)S(1)} fusion(f32[128,128]{1,0:T(8,128)S(1)} %fusion.13, s32[4096]{0:T(1024)S(1)} %reshape.43), kind=kCustom, calls=%fused_computation | custom fusion | bytes 65536 | tf_op jit(solution)/shard_map/jit(take_along_axis)/gather | solution.py:51
  285.7 54.5 %psum.15 = f32[128,32]{1,0:T(8,128)S(1)} all-reduce(f32[128,32]{1,0:T(8,128)S(1)} %select_select_fusion), channel_id=1, replica_groups=mesh['dp'=32,'table'=16] {'table'}, use_global_device_ids=true, to_apply=%region_7.8 | all-reduce | flops 4096 | bytes 32768 | tf_op jit(solution)/shard_map/psum | solution.py:53
  340.2 0.2 multiply_reduce_fusion
  340.5 0.7 copy.28
  341.2 43.4 %all-reduce.2.cloned.1.call-done = bf16[128,4096]{1,0:T(8,128)(2,1)} async-done(((bf16[128,4096]{1,0:T(8,128)(2,1)}), bf16[128,4096]{1,0:T(8,128)(2,1)}) %all-reduce.2.cloned.1.call-update) | async-done | bytes 1048592 | tf_op jit(solution)/shard_map/psum | solution.py:55
  384.5 2.8 convert_element_type.53
  387.3 102.8 %reduce-scatter.7.cloned.1.call-done = bf16[128,256]{1,0:T(8,128)(2,1)} async-done(((bf16[4096,256]{1,0:T(8,128)(2,1)}), bf16[128,256]{1,0:T(8,128)(2,1)}) %reduce-scatter.7.cloned.1.call-update) | async-done | bytes 65552
  490.1 0.9 copy.30
  491.0 0.8 copy.27
  491.8 72.0 %reduce-scatter.5.cloned.1.call-done = bf16[128,256]{1,0:T(8,128)(2,1)} async-done(((bf16[128,4096]{1,0:T(8,128)(2,1)}), bf16[128,256]{1,0:T(8,128)(2,1)}) %reduce-scatter.5.cloned.1.call-update) | async-done | bytes 65552 | tf_op jit(solution)/shard_map/reduce_scatter | solution.py:67
  (30 shorter events, 1.2 us)
Async XLA Ops:
  7.2 33.2 %copy-start = (bf16[128,4096]{1,0:T(8,128)(2,1)S(1)}, bf16[128,4096]{1,0:T(8,128)(2,1)}, u32[]{:S(2)}) copy-start(bf16[128,4096]{1,0:T(8,128)(2,1)} %param.8) | copy-start | bytes 3145732
  7.2 106.6 %all-gather.4.cloned.1.call-start = ((), (), s32[]{:S(2)}) async-start(), calls=%async_computation.3 | async-start | bytes 1114112 | tf_op jit(solution)/shard_map/all_gather | solution.py:25
  41.9 131.4 %copy-start.2 = (bf16[128,256]{1,0:T(8,128)(2,1)S(1)}, bf16[128,256]{1,0:T(8,128)(2,1)}, u32[]{:S(2)}) copy-start(bf16[128,256]{1,0:T(8,128)(2,1)} %param.11) | copy-start | bytes 196612
  41.9 70.5 %all-to-all-start = ((bf16[128,16,256]{2,0,1:T(8,128)(2,1)}), bf16[128,16,256]{2,0,1:T(8,128)(2,1)S(1)}, u32[]{:S(2)}, u32[]{:S(2)}) async-start(bf16[128,16,256]{2,0,1:T(8,128)(2,1)} %bitcast.27), calls=%async_computation | async-start | bytes 2097152 | tf_op jit(solution)/shard_map/all_to_all | solution.py:32
  57.2 116.1 %all-gather.6.cloned.1.call-start = ((), (), s32[]{:S(2)}) async-start(), calls=%async_computation.4 | async-start | bytes 2162688 | tf_op jit(solution)/shard_map/all_gather | solution.py:26
  58.0 190.6 %all-gather.8.cloned.1.call-start = ((), (), s32[]{:S(2)}) async-start(), calls=%async_computation.6 | async-start | bytes 1114112 | tf_op jit(solution)/shard_map/all_gather | solution.py:44
  176.4 208.2 %all-reduce.2.cloned.1.call-start = ((), (), s32[]{:S(2)}) async-start(), calls=%async_computation.7 | async-start | bytes 2097152 | tf_op jit(solution)/shard_map/psum | solution.py:55
  251.3 238.8 %reduce-scatter.7.cloned.1.call-start = ((), (), s32[]{:S(2)}) async-start(), calls=%async_computation.8 | async-start | bytes 2162688
  255.8 3.7 copy-start.1
  255.8 308.0 %reduce-scatter.5.cloned.1.call-start = ((), (), s32[]{:S(2)}) async-start(), calls=%async_computation.5 | async-start | bytes 1114112 | tf_op jit(solution)/shard_map/reduce_scatter | solution.py:67
Sparse Core Ops, SparseCore 0:
  10.0 103.7 all-gather.3
  116.9 56.3 all-gather.5
  176.5 72.0 all-gather.7
  252.2 132.2 all-reduce.1
  389.4 100.6 reduce-scatter.6
  493.6 70.2 reduce-scatter.4
where the time goes:
time: 571 us
  waiting for transfers between devices  407 us (71%)
  local copies, waits for them, and re-layouts  62.3 us (11%)
  blocking collectives  54.5 us (10%)
  starting transfers between devices  15.6 us (3%)
  between operations  14.3 us (3%)
  matrix products  12 us (2%)
    unnamed x7, waiting for transfers between devices  104 us
    all_gather x1, waiting for transfers between devices, local(): grad_full = lax.all_gather(mem_grad, 'table', axis=1, tiled=True)  72.2 us
    reduce_scatter x1, waiting for transfers between devices, local(): lax.psum_scatter(input_term.astype(jnp.bfloat16), 'table', scatter_dimens...  72 us
    all_gather x1, waiting for transfers between devices, local(): weight_full = lax.all_gather(gate_weight, 'dp', axis=0, tiled=True)  59.5 us
    psum x1, blocking collectives, local(): affinity = lax.psum(affinity_part, 'table')  54.5 us
    all_to_all x1, waiting for transfers between devices, local(): lax.all_to_all(partial_mem.astype(jnp.bfloat16), 'table', split_axis=1, c...  54.4 us
    psum x1, waiting for transfers between devices, local(): lax.psum(value_term.astype(jnp.bfloat16), 'dp').astype(jnp.float32)  43.4 us
    unnamed x15, local copies, waits for them, and re-layouts  35.3 us
  transfers between devices with their start and end apart: 7, of which 7 were waited for; matrix products, arithmetic and copies ran while one was open for 13% of the time, Pallas kernels for 0%

commit v1 on v0

--- a/solution.py
+++ b/solution.py
@@ -2,6 +2,27 @@
 import jax.numpy as jnp
 from jax import lax
 from jax.sharding import PartitionSpec as P
+
+
+def gather_around(x, axis, dim):
+    size, index, width = (lax.axis_size(axis), lax.axis_index(axis), x.shape[dim])
+    upward = [(i, (i + 1) % size) for i in range(size)]
+    left = [(i, (i - 1) % size) for i in range(size)]
+    out = jnp.zeros((*x.shape[:dim], size * width, *x.shape[dim + 1 :]), x.dtype)
+    out = lax.dynamic_update_slice_in_dim(out, x, index * width, axis=dim)
+    from_left = from_right = x
+    half = size // 2
+    for step in range(1, half + 1):
+        from_left = lax.ppermute(from_left, axis, upward)
+        out = lax.dynamic_update_slice_in_dim(
+            out, from_left, (index - step) % size * width, axis=dim
+        )
+        if step < size - half:
+            from_right = lax.ppermute(from_right, axis, left)
+            out = lax.dynamic_update_slice_in_dim(
+                out, from_right, (index + step) % size * width, axis=dim
+            )
+    return out
 
 
 def pick_weights(pick_scores):
@@ -41,7 +62,7 @@
     upstream = grad_out.astype(jnp.float32)
     mem_grad = (upstream * gate_value).astype(jnp.bfloat16)
     gate_grad_in = (upstream * memory_read * gate_slope).astype(jnp.bfloat16)
-    grad_full = lax.all_gather(mem_grad, "table", axis=1, tiled=True)
+    grad_full = gather_around(mem_grad, "table", 1)
     value_term = lax.dot_general(
         spread, grad_full, (((0,), (0,)), ((), ())), preferred_element_type=jnp.float32
     )

time: 571 us -> 654 us (1.15)
  starting transfers between devices: 15.6 us -> 62.6 us
  waiting for transfers between devices: 407 us -> 445 us
    all_gather x1, waiting for transfers between devices: 1.23 us -> 74.2 us  [local(): whole_in = lax.all_gather(hidden_in, 'table', axis=1, tiled=True)]
    all_gather x1 -> x0, waiting for transfers between devices: 72.2 us -> none  [local(): grad_full = lax.all_gather(mem_grad, 'table', axis=1, tiled=True)]
    psum x1, waiting for transfers between devices: 43.4 us -> 97.7 us  [local(): lax.psum(value_term.astype(jnp.bfloat16), 'dp').astype(jnp.float32)]
    ppermute x0 -> x15, starting transfers between devices: none -> 52 us  [the longest x7 35.2 us: gather_around(): from_right = lax.ppermute(from_right, axis, left)]
    all_to_all x1, waiting for transfers between devices: 54.4 us -> 31.6 us  [local(): lax.all_to_all(partial_mem.astype(jnp.bfloat16), 'table', split_axis=1, c...]
    ppermute x0 -> x15, waiting for transfers between devices: none -> 7.29 us  [the longest x8 7.27 us: gather_around(): from_left = lax.ppermute(from_left, axis, upward)]
    unnamed x7 -> x6, waiting for transfers between devices: 104 us -> 104 us
  transfers between devices with their start and end apart: 7 -> 21, of which waited for: 7 -> 14; matrix products, arithmetic and copies ran while one was open for 13% -> 3% of each run, Pallas kernels for 0% -> 0%
where the time goes in v1:
time: 654 us
  waiting for transfers between devices  445 us (68%)
  local copies, waits for them, and re-layouts  64.1 us (10%)
  starting transfers between devices  62.6 us (10%)
  blocking collectives  53.5 us (8%)
  between operations  14.6 us (2%)
  matrix products  8.43 us (1%)
    unnamed x6, waiting for transfers between devices  104 us
    psum x1, waiting for transfers between devices, local(): lax.psum(value_term.astype(jnp.bfloat16), 'dp').astype(jnp.float32)  97.7 us
    all_gather x1, waiting for transfers between devices, local(): whole_in = lax.all_gather(hidden_in, 'table', axis=1, tiled=True)  74.2 us
    reduce_scatter x1, waiting for transfers between devices, local(): lax.psum_scatter(input_term.astype(jnp.bfloat16), 'table', scatter_dimens...  72 us
    all_gather x1, waiting for transfers between devices, local(): weight_full = lax.all_gather(gate_weight, 'dp', axis=0, tiled=True)  57.7 us
    psum x1, blocking collectives, local(): affinity = lax.psum(affinity_part, 'table')  53.5 us
    unnamed x15, local copies, waits for them, and re-layouts  36.8 us
    ppermute x7, starting transfers between devices, gather_around(): from_right = lax.ppermute(from_right, axis, left)  35.2 us
  transfers between devices with their start and end apart: 21, of which 14 were waited for; matrix products, arithmetic and copies ran while one was open for 3% of the time, Pallas kernels for 0%

profile of v1, /device:TPU:6, one launch (start us, length us, event | category | flops | bytes accessed | tf_op | source)
XLA Modules:
  0.0 653.5 jit_solution(14077035180981401080)
XLA Ops:
  12.6 74.2 %all-gather.3.cloned.1.call-done = bf16[128,4096]{1,0:T(8,128)(2,1)} async-done(((bf16[128,256]{1,0:T(8,128)(2,1)}), bf16[128,4096]{1,0:T(8,128)(2,1)}) %all-gather.3.cloned.1.call-update) | async-done | bytes 1048592 | tf_op jit(solution)/shard_map/all_gather | solution.py:46
  86.7 57.7 %all-gather.5.cloned.1.call-done = bf16[4096,256]{1,0:T(8,128)(2,1)} async-done(((bf16[128,256]{1,0:T(8,128)(2,1)}), bf16[4096,256]{1,0:T(8,128)(2,1)}) %all-gather.5.cloned.1.call-update) | async-done | bytes 2097168 | tf_op jit(solution)/shard_map/all_gather | solution.py:47
  144.6 2.4 constant_dynamic-update-slice_fusion.15
  147.0 3.5 collective-permute-start
  150.4 4.4 collective-permute-start.1
  155.4 1.9 collective-permute-start.2
  157.3 5.1 collective-permute-start.3
  162.8 1.9 collective-permute-start.4
  164.7 5.1 collective-permute-start.5
  170.1 1.9 collective-permute-start.6
  172.1 5.1 collective-permute-start.7
  177.5 1.9 collective-permute-start.8
  179.4 5.1 collective-permute-start.9
  184.8 1.9 collective-permute-start.10
  186.8 5.1 collective-permute-start.11
  192.2 1.9 collective-permute-start.12
  194.1 5.1 collective-permute-start.13
  199.6 1.9 collective-permute-start.14
  201.5 5.4 collective-permute-done.14
  207.4 25.6 %gather_fusion = f32[4096]{0:T(1024)S(1)} fusion(f32[128,128]{1,0:T(8,128)S(1)} %fusion.14, s32[4096]{0:T(1024)S(1)} %reshape.43), kind=kCustom, calls=%fused_computation | custom fusion | bytes 65536 | tf_op jit(solution)/shard_map/jit(take_along_axis)/gather | solution.py:72
  233.1 53.5 %psum.15 = f32[128,32]{1,0:T(8,128)S(1)} all-reduce(f32[128,32]{1,0:T(8,128)S(1)} %select_select_fusion), channel_id=1, replica_groups=mesh['dp'=32,'table'=16] {'table'}, use_global_device_ids=true, to_apply=%region_7.8 | all-reduce | flops 4096 | bytes 32768 | tf_op jit(solution)/shard_map/psum | solution.py:74
  287.1 28.6 %scatter_custom_fusion = bf16[16384]{0:T(1024)(128)(2,1)S(1)} fusion(s32[4096]{0:T(1024)S(1)} %reshape.49, bf16[4096]{0:T(1024)(128)(2,1)S(1)} %reshape.51, bf16[]{:T(256)} %constant.110.clone.1), kind=kCustom, calls=%fused_computation.33 | custom fusion | bytes 32770
  317.2 10.4 %all-to-all-start = ((bf16[128,16,256]{2,0,1:T(8,128)(2,1)}), bf16[128,16,256]{2,0,1:T(8,128)(2,1)S(1)}, u32[]{:S(2)}, u32[]{:S(2)}) async-start(bf16[128,16,256]{2,0,1:T(8,128)(2,1)} %bitcast.29), calls=%async_computation | async-start | bytes 2097152 | tf_op jit(solution)/shard_map/all_to_all | solution.py:53
  329.1 31.6 %all-to-all-done = bf16[128,16,256]{2,0,1:T(8,128)(2,1)S(1)} async-done(((bf16[128,16,256]{2,0,1:T(8,128)(2,1)}), bf16[128,16,256]{2,0,1:T(8,128)(2,1)S(1)}, u32[]{:S(2)}, u32[]{:S(2)}) %all-to-all-start) | async-done | bytes 1048608 | tf_op jit(solution)/shard_map/all_to_all | solution.py:53
  361.5 1.9 fusion
  363.5 2.5 copy.29
  366.1 1.5 copy-done.1
  367.6 1.8 convolution_convert_fusion.2
  370.1 97.7 %all-reduce.2.cloned.1.call-done = bf16[128,4096]{1,0:T(8,128)(2,1)} async-done(((bf16[128,4096]{1,0:T(8,128)(2,1)}), bf16[128,4096]{1,0:T(8,128)(2,1)}) %all-reduce.2.cloned.1.call-update) | async-done | bytes 1048592 | tf_op jit(solution)/shard_map/psum | solution.py:76
  467.8 2.8 convert_element_type.53
  470.5 102.8 %reduce-scatter.7.cloned.1.call-done = bf16[128,256]{1,0:T(8,128)(2,1)} async-done(((bf16[4096,256]{1,0:T(8,128)(2,1)}), bf16[128,256]{1,0:T(8,128)(2,1)}) %reduce-scatter.7.cloned.1.call-update) | async-done | bytes 65552
  575.0 72.0 %reduce-scatter.5.cloned.1.call-done = bf16[128,256]{1,0:T(8,128)(2,1)} async-done(((bf16[128,4096]{1,0:T(8,128)(2,1)}), bf16[128,256]{1,0:T(8,128)(2,1)}) %reduce-scatter.5.cloned.1.call-update) | async-done | bytes 65552 | tf_op jit(solution)/shard_map/reduce_scatter | solution.py:88
  (73 shorter events, 14.7 us)
Async XLA Ops:
  7.2 199.8 %copy-start = (bf16[128,4096]{1,0:T(8,128)(2,1)S(1)}, bf16[128,4096]{1,0:T(8,128)(2,1)}, u32[]{:S(2)}) copy-start(bf16[128,4096]{1,0:T(8,128)(2,1)} %param.8) | copy-start | bytes 3145732
  7.2 137.4 %copy-start.2 = (bf16[128,256]{1,0:T(8,128)(2,1)S(1)}, bf16[128,256]{1,0:T(8,128)(2,1)}, u32[]{:S(2)}) copy-start(bf16[128,256]{1,0:T(8,128)(2,1)} %param.11) | copy-start | bytes 196612
  7.2 79.6 %all-gather.3.cloned.1.call-start = ((), (), s32[]{:S(2)}) async-start(), calls=%async_computation.3 | async-start | bytes 1114112 | tf_op jit(solution)/shard_map/all_gather | solution.py:46
  7.9 136.5 %all-gather.5.cloned.1.call-start = ((), (), s32[]{:S(2)}) async-start(), calls=%async_computation.4 | async-start | bytes 2162688 | tf_op jit(solution)/shard_map/all_gather | solution.py:47
  147.0 8.5 %collective-permute-start = (bf16[128,256]{1,0:T(8,128)(2,1)S(1)}, bf16[128,256]{1,0:T(8,128)(2,1)S(1)}, u32[]{:S(2)}, u32[]{:S(2)}) collective-permute-start(bf16[128,256]{1,0:T(8,128)(2,1)S(1)} %get-tuple-element.26), channel_id=1, source_target_pairs={{0,1},{1,2},{2,3},{3,4},{4,5},{5,6},{6,7},{7,8},{8,9},{9,10},{10,1... | collective-permute-start | bytes 196616 | tf_op jit(solution)/shard_map/ppermute | solution.py:16
  150.4 6.9 %collective-permute-start.1 = (bf16[128,256]{1,0:T(8,128)(2,1)S(1)}, bf16[128,256]{1,0:T(8,128)(2,1)S(1)}, u32[]{:S(2)}, u32[]{:S(2)}) collective-permute-start(bf16[128,256]{1,0:T(8,128)(2,1)S(1)} %get-tuple-element.26), channel_id=1, source_target_pairs={{0,15},{1,0},{2,1},{3,2},{4,3},{5,4},{6,5},{7,6},{8,7},{9,8},{10,9... | collective-permute-start | bytes 196616 | tf_op jit(solution)/shard_map/ppermute | solution.py:21
  155.4 7.4 %collective-permute-start.2 = (bf16[128,256]{1,0:T(8,128)(2,1)S(1)}, bf16[128,256]{1,0:T(8,128)(2,1)S(1)}, u32[]{:S(2)}, u32[]{:S(2)}) collective-permute-start(bf16[128,256]{1,0:T(8,128)(2,1)S(1)} %collective-permute-done), channel_id=1, source_target_pairs={{0,1},{1,2},{2,3},{3,4},{4,5},{5,6},{6,7},{7,8},{8,9},{9,10},{10,1... | collective-permute-start | bytes 196616 | tf_op jit(solution)/shard_map/ppermute | solution.py:16
  157.3 7.4 %collective-permute-start.3 = (bf16[128,256]{1,0:T(8,128)(2,1)S(1)}, bf16[128,256]{1,0:T(8,128)(2,1)S(1)}, u32[]{:S(2)}, u32[]{:S(2)}) collective-permute-start(bf16[128,256]{1,0:T(8,128)(2,1)S(1)} %collective-permute-done.1), channel_id=1, source_target_pairs={{0,15},{1,0},{2,1},{3,2},{4,3},{5,4},{6,5},{7,6},{8,7},{9,8},{10,9... | collective-permute-start | bytes 196616 | tf_op jit(solution)/shard_map/ppermute | solution.py:21
  162.8 7.4 %collective-permute-start.4 = (bf16[128,256]{1,0:T(8,128)(2,1)S(1)}, bf16[128,256]{1,0:T(8,128)(2,1)S(1)}, u32[]{:S(2)}, u32[]{:S(2)}) collective-permute-start(bf16[128,256]{1,0:T(8,128)(2,1)S(1)} %collective-permute-done.2), channel_id=1, source_target_pairs={{0,1},{1,2},{2,3},{3,4},{4,5},{5,6},{6,7},{7,8},{8,9},{9,10},{10,1... | collective-permute-start | bytes 196616 | tf_op jit(solution)/shard_map/ppermute | solution.py:16
  164.7 7.4 %collective-permute-start.5 = (bf16[128,256]{1,0:T(8,128)(2,1)S(1)}, bf16[128,256]{1,0:T(8,128)(2,1)S(1)}, u32[]{:S(2)}, u32[]{:S(2)}) collective-permute-start(bf16[128,256]{1,0:T(8,128)(2,1)S(1)} %collective-permute-done.3), channel_id=1, source_target_pairs={{0,15},{1,0},{2,1},{3,2},{4,3},{5,4},{6,5},{7,6},{8,7},{9,8},{10,9... | collective-permute-start | bytes 196616 | tf_op jit(solution)/shard_map/ppermute | solution.py:21
  170.1 7.4 %collective-permute-start.6 = (bf16[128,256]{1,0:T(8,128)(2,1)S(1)}, bf16[128,256]{1,0:T(8,128)(2,1)S(1)}, u32[]{:S(2)}, u32[]{:S(2)}) collective-permute-start(bf16[128,256]{1,0:T(8,128)(2,1)S(1)} %collective-permute-done.4), channel_id=1, source_target_pairs={{0,1},{1,2},{2,3},{3,4},{4,5},{5,6},{6,7},{7,8},{8,9},{9,10},{10,1... | collective-permute-start | bytes 196616 | tf_op jit(solution)/shard_map/ppermute | solution.py:16
  172.1 7.4 %collective-permute-start.7 = (bf16[128,256]{1,0:T(8,128)(2,1)S(1)}, bf16[128,256]{1,0:T(8,128)(2,1)S(1)}, u32[]{:S(2)}, u32[]{:S(2)}) collective-permute-start(bf16[128,256]{1,0:T(8,128)(2,1)S(1)} %collective-permute-done.5), channel_id=1, source_target_pairs={{0,15},{1,0},{2,1},{3,2},{4,3},{5,4},{6,5},{7,6},{8,7},{9,8},{10,9... | collective-permute-start | bytes 196616 | tf_op jit(solution)/shard_map/ppermute | solution.py:21
  177.5 7.4 %collective-permute-start.8 = (bf16[128,256]{1,0:T(8,128)(2,1)S(1)}, bf16[128,256]{1,0:T(8,128)(2,1)S(1)}, u32[]{:S(2)}, u32[]{:S(2)}) collective-permute-start(bf16[128,256]{1,0:T(8,128)(2,1)S(1)} %collective-permute-done.6), channel_id=1, source_target_pairs={{0,1},{1,2},{2,3},{3,4},{4,5},{5,6},{6,7},{7,8},{8,9},{9,10},{10,1... | collective-permute-start | bytes 196616 | tf_op jit(solution)/shard_map/ppermute | solution.py:16
  179.4 7.4 %collective-permute-start.9 = (bf16[128,256]{1,0:T(8,128)(2,1)S(1)}, bf16[128,256]{1,0:T(8,128)(2,1)S(1)}, u32[]{:S(2)}, u32[]{:S(2)}) collective-permute-start(bf16[128,256]{1,0:T(8,128)(2,1)S(1)} %collective-permute-done.7), channel_id=1, source_target_pairs={{0,15},{1,0},{2,1},{3,2},{4,3},{5,4},{6,5},{7,6},{8,7},{9,8},{10,9... | collective-permute-start | bytes 196616 | tf_op jit(solution)/shard_map/ppermute | solution.py:21
  184.8 7.4 %collective-permute-start.10 = (bf16[128,256]{1,0:T(8,128)(2,1)S(1)}, bf16[128,256]{1,0:T(8,128)(2,1)S(1)}, u32[]{:S(2)}, u32[]{:S(2)}) collective-permute-start(bf16[128,256]{1,0:T(8,128)(2,1)S(1)} %collective-permute-done.8), channel_id=1, source_target_pairs={{0,1},{1,2},{2,3},{3,4},{4,5},{5,6},{6,7},{7,8},{8,9},{9,10},{10,1... | collective-permute-start | bytes 196616 | tf_op jit(solution)/shard_map/ppermute | solution.py:16
  186.8 7.4 %collective-permute-start.11 = (bf16[128,256]{1,0:T(8,128)(2,1)S(1)}, bf16[128,256]{1,0:T(8,128)(2,1)S(1)}, u32[]{:S(2)}, u32[]{:S(2)}) collective-permute-start(bf16[128,256]{1,0:T(8,128)(2,1)S(1)} %collective-permute-done.9), channel_id=1, source_target_pairs={{0,15},{1,0},{2,1},{3,2},{4,3},{5,4},{6,5},{7,6},{8,7},{9,8},{10,9... | collective-permute-start | bytes 196616 | tf_op jit(solution)/shard_map/ppermute | solution.py:21
  192.2 7.4 %collective-permute-start.12 = (bf16[128,256]{1,0:T(8,128)(2,1)S(1)}, bf16[128,256]{1,0:T(8,128)(2,1)S(1)}, u32[]{:S(2)}, u32[]{:S(2)}) collective-permute-start(bf16[128,256]{1,0:T(8,128)(2,1)S(1)} %collective-permute-done.10), channel_id=1, source_target_pairs={{0,1},{1,2},{2,3},{3,4},{4,5},{5,6},{6,7},{7,8},{8,9},{9,10},{10,1... | collective-permute-start | bytes 196616 | tf_op jit(solution)/shard_map/ppermute | solution.py:16
  194.1 7.4 %collective-permute-start.13 = (bf16[128,256]{1,0:T(8,128)(2,1)S(1)}, bf16[128,256]{1,0:T(8,128)(2,1)S(1)}, u32[]{:S(2)}, u32[]{:S(2)}) collective-permute-start(bf16[128,256]{1,0:T(8,128)(2,1)S(1)} %collective-permute-done.11), channel_id=1, source_target_pairs={{0,15},{1,0},{2,1},{3,2},{4,3},{5,4},{6,5},{7,6},{8,7},{9,8},{10,9... | collective-permute-start | bytes 196616 | tf_op jit(solution)/shard_map/ppermute | solution.py:21
  199.6 7.4 %collective-permute-start.14 = (bf16[128,256]{1,0:T(8,128)(2,1)S(1)}, bf16[128,256]{1,0:T(8,128)(2,1)S(1)}, u32[]{:S(2)}, u32[]{:S(2)}) collective-permute-start(bf16[128,256]{1,0:T(8,128)(2,1)S(1)} %collective-permute-done.12), channel_id=1, source_target_pairs={{0,1},{1,2},{2,3},{3,4},{4,5},{5,6},{6,7},{7,8},{8,9},{9,10},{10,1... | collective-permute-start | bytes 196616 | tf_op jit(solution)/shard_map/ppermute | solution.py:16
  317.2 43.5 %all-to-all-start = ((bf16[128,16,256]{2,0,1:T(8,128)(2,1)}), bf16[128,16,256]{2,0,1:T(8,128)(2,1)S(1)}, u32[]{:S(2)}, u32[]{:S(2)}) async-start(bf16[128,16,256]{2,0,1:T(8,128)(2,1)} %bitcast.29), calls=%async_computation | async-start | bytes 2097152 | tf_op jit(solution)/shard_map/all_to_all | solution.py:53
  327.6 140.2 %all-reduce.2.cloned.1.call-start = ((), (), s32[]{:S(2)}) async-start(), calls=%async_computation.6 | async-start | bytes 2097152 | tf_op jit(solution)/shard_map/psum | solution.py:76
  329.1 244.2 %reduce-scatter.7.cloned.1.call-start = ((), (), s32[]{:S(2)}) async-start(), calls=%async_computation.7 | async-start | bytes 2162688
  366.0 1.6 copy-start.1
  366.0 281.0 %reduce-scatter.5.cloned.1.call-start = ((), (), s32[]{:S(2)}) async-start(), calls=%async_computation.5 | async-start | bytes 1114112 | tf_op jit(solution)/shard_map/reduce_scatter | solution.py:88
Sparse Core Ops, SparseCore 0:
  10.0 76.6 all-gather.2
  89.9 54.5 all-gather.4
  331.6 136.1 all-reduce.1
  472.7 100.5 reduce-scatter.6
  576.8 70.1 reduce-scatter.4
